TPU v7x, 32 devices: a whole 2x2x4 slice. The times are simulated.
32 devices in a mesh: rep: 2 (over x), seq: 16 (over z, y, core).
Axes of the slice: x: 2, y: 2, z: 4, core: 2. Of those that a mesh axis runs over, the one named last changes fastest.
Arguments:
- projected: bfloat16 [24576, 4096], P(('rep', 'seq')), parts along dimension 0, may hold values from -6 to 6
- history_in: bfloat16 [24576, 1024], P(('rep', 'seq')), parts along dimension 0, may hold values from -6 to 6
- norm_gain: float32 [1024], replicated, may hold values from 0.1 to 1.9
- out_proj: bfloat16 [1024, 1024], replicated, may hold values from -0.1875 to 0.1875
- user_spans: int32 [16], P('rep'), parts along dimension 0, may hold values from 1 to 4, as said below
- user_tails: int32 [16], P('rep'), parts along dimension 0, may hold values from 1 to 768
- cand_emb: bfloat16 [4096, 1024], P(('rep', 'seq')), parts along dimension 0, may hold values from -6 to 6
- cand_user: int32 [4096], P(('rep', 'seq')), parts along dimension 0, may hold values from 0 to 7
- cross_down: bfloat16 [2048, 128], replicated, may hold values from -0.125 to 0.125
- cross_up: bfloat16 [128, 2048], replicated, may hold values from -0.5 to 0.5
- cross_bias: float32 [2048], replicated, may hold values from -4 to 4
- score_weight: float32 [2048], replicated, may hold values from -0.125 to 0.125
Outputs:
- history_out: bfloat16 [24576, 1024], P(('rep', 'seq')), parts along dimension 0
- scores: float32 [4096], P(('rep', 'seq')), parts along dimension 0
There are 2 independent parts, one for each index of `rep`. A program takes and returns all parts, laid end to end along the dimension named above; an argument that names none is the same for every part. Nothing has to cross between parts.
Inputs may be any that keep to these rules, and one draw needn't show every extreme that they name: `user_spans`: users own consecutive segments in order and together own all 16 segments; some user owns exactly 4.
All inputs are finite; a program needn't handle non-finite values.
Results may differ from a plain program's by a relative error of at most 0.0059.
Values may be sent and summed in bfloat16 or wider, within the bound.
A program may use at most 128 MiB of HBM per device.

v0:
```python
import jax
import jax.numpy as jnp
from jax import lax
from jax.sharding import PartitionSpec as P

HEADS = 8


def shifted(x, axis, by):
    peers = lax.axis_size(axis)
    pairs = [(i, i + by) for i in range(peers) if 0 <= i + by < peers]
    return lax.ppermute(x, axis, pairs)


def attend(totals, queries, key_values, weight_mask, score_scale):
    key_count = key_values.shape[0]
    model_width = key_values.shape[1] // 2
    head_count = queries.shape[1]
    key_part = key_values[:, :model_width].reshape(key_count, head_count, -1)
    value_part = key_values[:, model_width:].reshape(key_count, head_count, -1)
    logits = (
        jnp.einsum("qhd,khd->hqk", queries, key_part, preferred_element_type=jnp.float32)
        * score_scale
    )
    weights = (jax.nn.silu(logits) * weight_mask).astype(jnp.bfloat16)
    return totals + jnp.einsum(
        "hqk,khd->qhd", weights, value_part, preferred_element_type=jnp.float32
    )


def body(
    projected,
    history_in,
    norm_gain,
    out_proj,
    user_spans,
    user_tails,
    cand_emb,
    cand_user,
    cross_down,
    cross_up,
    cross_bias,
    score_weight,
):
    row_count, model_width = history_in.shape
    head_size = model_width // HEADS
    score_scale = head_size ** (-0.5)
    devices = lax.axis_size("seq")
    my_index = lax.axis_index("seq")
    span_limit = min(4, devices // 2)
    last_dev = jnp.cumsum(user_spans) - 1
    first_dev = last_dev - user_spans + 1
    device_ids = jnp.arange(devices, dtype=jnp.int32)
    owner_of = jnp.sum((first_dev[None, :] <= device_ids[:, None]).astype(jnp.int32), axis=1) - 1
    is_end = device_ids == last_dev[owner_of]
    valid_rows = jnp.where(is_end, user_tails[owner_of], row_count)
    queries = projected[:, model_width : 2 * model_width].reshape(row_count, HEADS, head_size)
    own_block = projected[:, 2 * model_width :]
    row_ids = jnp.arange(row_count, dtype=jnp.int32)
    causal = (row_ids[None, :] <= row_ids[:, None]).astype(jnp.float32)
    totals = attend(
        jnp.zeros((row_count, HEADS, head_size), jnp.float32),
        queries,
        own_block,
        causal,
        score_scale,
    )

    def add_block(totals, key_values, offset):
        source = my_index - offset
        same_user = (source >= 0) & (owner_of[jnp.maximum(source, 0)] == owner_of[my_index])
        result = lax.cond(
            same_user,
            lambda current: attend(current, queries, key_values, jnp.float32(1.0), score_scale),
            lambda current: current,
            totals,
        )
        return result

    def next_block(offset, loop_state):
        totals, moving = loop_state
        moving = shifted(moving, "seq", 1)
        return (add_block(totals, moving, offset), moving)

    totals, moving = lax.fori_loop(1, span_limit, next_block, (totals, own_block))
    valid_here = valid_rows[my_index]
    row_valid = (row_ids < valid_here).astype(jnp.float32)
    attention = totals.reshape(row_count, model_width) * row_valid[:, None]
    row_mean = jnp.mean(attention, axis=1, keepdims=True)
    centered = attention - row_mean
    row_var = jnp.mean(centered * centered, axis=1, keepdims=True)
    normed = centered * lax.rsqrt(row_var + 1e-06) * norm_gain
    gated = (normed * projected[:, :model_width].astype(jnp.float32)).astype(jnp.bfloat16)
    history_out = (
        jnp.dot(gated, out_proj, preferred_element_type=jnp.float32)
        + history_in.astype(jnp.float32)
    ).astype(jnp.bfloat16)
    last_row = jnp.where(is_end[my_index], valid_here - 1, 0)
    final_row = lax.dynamic_slice_in_dim(history_out, last_row, 1, 0)
    final_row = jnp.where(is_end[my_index], final_row, jnp.zeros_like(final_row))
    user_rows = lax.all_gather(final_row, "seq", axis=0, tiled=True)
    user_count = user_spans.shape[0]
    user_match = cand_user[:, None] == jnp.arange(user_count, dtype=jnp.int32)[None, :]
    cand_dev = jnp.sum(jnp.where(user_match, last_dev[None, :], 0), axis=1)
    selector = (cand_dev[:, None] == device_ids[None, :]).astype(jnp.bfloat16)
    user_part = jnp.dot(selector, user_rows, preferred_element_type=jnp.float32).astype(
        jnp.bfloat16
    )
    crossed_in = jnp.concatenate([user_part, cand_emb], axis=1)
    low_rank = jnp.dot(crossed_in, cross_down, preferred_element_type=jnp.float32).astype(
        jnp.bfloat16
    )
    up_part = jnp.dot(low_rank, cross_up, preferred_element_type=jnp.float32)
    input_float = crossed_in.astype(jnp.float32)
    crossed = input_float * (up_part + cross_bias) + input_float
    scores = jnp.sum(crossed * score_weight, axis=1)
    return (history_out, scores)


def solution(mesh):
    in_specs = (
        P(("rep", "seq"), None),
        P(("rep", "seq"), None),
        P(),
        P(),
        P("rep"),
        P("rep"),
        P(("rep", "seq"), None),
        P(("rep", "seq")),
        P(),
        P(),
        P(),
        P(),
    )
    out_specs = (P(("rep", "seq"), None), P(("rep", "seq")))
    return jax.shard_map(body, mesh=mesh, in_specs=in_specs, out_specs=out_specs, check_vma=False)
```

profile of v0, /device:TPU:3, one launch (start us, length us, event | category | flops | bytes accessed | tf_op | source)
XLA Modules:
  0.0 262.3 jit_solution(10896016889106156357)
XLA Ops:
  0.6 0.0 copy-start
  0.6 1.0 reduce-window.7
  1.6 0.0 copy-start.10
  1.6 0.7 subtract_add_fusion
  2.3 0.1 convert_reduce_fusion
  2.4 0.0 copy-start.12
  2.4 0.5 copy-done.12
  2.9 0.6 dynamic_slice.28
  3.5 5.7 %fusion.36 = (bf16[768,1024]{1,0:T(8,128)(2,1)}, bf16[768,1024]{1,0:T(8,128)(2,1)}, bf16[768,1024]{1,0:T(8,128)(2,1)}, bf16[768,1024]{1,0:T(8,128)(2,1)}) fusion(bf16[768,4096]{1,0:T(8,128)(2,1)} %param.16), kind=kLoop, calls=%fused_computation.59 | loop fusion | bytes 12582912 | tf_op jit(solution)/shard_map/slice | solution.py:93
  9.2 0.0 copy-done.10
  9.2 2.6 copy.56
  11.8 2.7 %copy.57 = bf16[768,1024]{0,1:T(8,128)(2,1)} copy(bf16[768,1024]{1,0:T(8,128)(2,1)} %get-tuple-element.218) | data formatting | bytes 3145728
  14.4 2.6 copy.58
  17.0 1.6 fusion.16
  18.6 12.1 %fusion.17 = f32[768,8,128]{2,0,1:T(8,128)} fusion(bf16[768,8,128]{0,2,1:T(8,128)(2,1)} %bitcast.57, f32[768,768]{1,0:T(8,128)} %fusion.16, bf16[768,8,128]{0,2,1:T(8,128)(2,1)} %bitcast.54, bf16[768,8,128]{0,2,1:T(8,128)(2,1)} %bitcast.56), kind=kOutput, calls=%fused_computation.26 | convolution fusion | flops 2448949248 | bytes 10223616 | tf_op jit(solution)/shard_map/hqk,khd->qhd/dot_general | solution.py:26
  30.7 2.6 copy.47
  33.3 4.0 %slice.26 = bf16[768,2048]{1,0:T(8,128)(2,1)} slice(bf16[768,4096]{1,0:T(8,128)(2,1)} %param.16), slice={[0:768], [2048:4096]} | slice | bytes 6291456 | tf_op jit(solution)/shard_map/slice | solution.py:58
  37.2 4.7 %copy.59 = bf16[768,2048]{0,1:T(8,128)(2,1)} copy(bf16[768,2048]{1,0:T(8,128)(2,1)} %slice.26) | data formatting | bytes 6291456
  42.0 142.6 %while.20 = (s32[]{:T(128)}, f32[768,8,128]{2,0,1:T(8,128)}, bf16[768,2048]{0,1:T(8,128)(2,1)}, s32[]{:T(128)}, s32[16]{0:T(128)S(1)}, /*index=5*/s32[1]{0:T(128)}, bf16[768,8,128]{2,0,1:T(8,128)(2,1)}, s32[]{:T(128)}, s32[]{:T(128)}) while((s32[]{:T(128)}, f32[768,8,128]{2,0,1:T(8,128)}, bf16[768,2048]{0,1:T(8,128)(2,1)}, s32[]{:T(128)}, ...), condition=%wide.region_5.6_spmd, body=%wide.region_2.5_spmd.sunk | while | flops 2445017088 | bytes 36176096 | solution.py:85
  42.0 3.7 %collective-permute-start = (bf16[768,2048]{0,1:T(8,128)(2,1)}, bf16[768,2048]{0,1:T(8,128)(2,1)}, u32[]{:S(2)}, u32[]{:S(2)}) collective-permute-start(bf16[768,2048]{0,1:T(8,128)(2,1)} %get-tuple-element.274), channel_id=1, source_target_pairs={{0,1},{1,2},{2,3},{3,4},{4,5},{5,6},{6,7},{7,8},{8,9},{9,10},{10,1... | collective-permute-start | bytes 9437192 | tf_op jit(solution)/shard_map/while/body/eval_jaxpr/ppermute | solution.py:12
  45.7 0.6 dynamic_slice.34
  47.5 32.7 %collective-permute-done = bf16[768,2048]{0,1:T(8,128)(2,1)} collective-permute-done((bf16[768,2048]{0,1:T(8,128)(2,1)}, bf16[768,2048]{0,1:T(8,128)(2,1)}, u32[]{:S(2)}, u32[]{:S(2)}) %collective-permute-start) | collective-permute-done | bytes 3145760 | tf_op jit(solution)/shard_map/while/body/eval_jaxpr/ppermute | solution.py:12
  80.2 3.8 %copy.75 = bf16[768,2048]{0,1:T(8,128)(2,1)} copy(bf16[768,2048]{0,1:T(8,128)(2,1)} %collective-permute-done) | data formatting | bytes 6291456 | tf_op jit(solution)/shard_map/while
  84.0 19.6 %collective-permute-start = (bf16[768,2048]{0,1:T(8,128)(2,1)}, bf16[768,2048]{0,1:T(8,128)(2,1)}, u32[]{:S(2)}, u32[]{:S(2)}) collective-permute-start(bf16[768,2048]{0,1:T(8,128)(2,1)} %get-tuple-element.274), channel_id=1, source_target_pairs={{0,1},{1,2},{2,3},{3,4},{4,5},{5,6},{6,7},{7,8},{8,9},{9,10},{10,1... | collective-permute-start | bytes 9437192 | tf_op jit(solution)/shard_map/while/body/eval_jaxpr/ppermute | solution.py:12
  103.6 0.6 dynamic_slice.34
  105.4 32.7 %collective-permute-done = bf16[768,2048]{0,1:T(8,128)(2,1)} collective-permute-done((bf16[768,2048]{0,1:T(8,128)(2,1)}, bf16[768,2048]{0,1:T(8,128)(2,1)}, u32[]{:S(2)}, u32[]{:S(2)}) %collective-permute-start) | collective-permute-done | bytes 3145760 | tf_op jit(solution)/shard_map/while/body/eval_jaxpr/ppermute | solution.py:12
  138.1 3.8 %copy.75 = bf16[768,2048]{0,1:T(8,128)(2,1)} copy(bf16[768,2048]{0,1:T(8,128)(2,1)} %collective-permute-done) | data formatting | bytes 6291456 | tf_op jit(solution)/shard_map/while
  141.9 4.4 %collective-permute-start = (bf16[768,2048]{0,1:T(8,128)(2,1)}, bf16[768,2048]{0,1:T(8,128)(2,1)}, u32[]{:S(2)}, u32[]{:S(2)}) collective-permute-start(bf16[768,2048]{0,1:T(8,128)(2,1)} %get-tuple-element.274), channel_id=1, source_target_pairs={{0,1},{1,2},{2,3},{3,4},{4,5},{5,6},{6,7},{7,8},{8,9},{9,10},{10,1... | collective-permute-start | bytes 9437192 | tf_op jit(solution)/shard_map/while/body/eval_jaxpr/ppermute | solution.py:12
  146.3 0.6 dynamic_slice.34
  148.1 32.7 %collective-permute-done = bf16[768,2048]{0,1:T(8,128)(2,1)} collective-permute-done((bf16[768,2048]{0,1:T(8,128)(2,1)}, bf16[768,2048]{0,1:T(8,128)(2,1)}, u32[]{:S(2)}, u32[]{:S(2)}) %collective-permute-start) | collective-permute-done | bytes 3145760 | tf_op jit(solution)/shard_map/while/body/eval_jaxpr/ppermute | solution.py:12
  180.8 3.8 %copy.75 = bf16[768,2048]{0,1:T(8,128)(2,1)} copy(bf16[768,2048]{0,1:T(8,128)(2,1)} %collective-permute-done) | data formatting | bytes 6291456 | tf_op jit(solution)/shard_map/while
  184.6 0.0 copy-done.13
  184.6 0.0 copy-done.11
  184.6 0.7 gather_fusion
  185.3 0.0 copy-done.1
  185.3 0.7 gather_fusion.1
  186.0 0.6 dynamic_slice.29
  186.5 0.9 fusion.29
  187.5 2.2 multiply_reduce_fusion.1
  189.7 0.0 copy-done.2
  189.8 0.6 multiply_reduce_fusion
  190.4 3.7 %copy.48 = f32[768,8,128]{0,2,1:T(8,128)} copy(f32[768,8,128]{2,0,1:T(8,128)} %get-tuple-element.178) | data formatting | bytes 6291456 | tf_op jit(solution)/shard_map/while | solution.py:85
  194.1 2.6 copy.60
  196.7 0.0 copy-done.3
  196.7 3.2 %fusion.12 = bf16[768,1024]{0,1:T(8,128)(2,1)S(1)} fusion(f32[768,8,128]{0,2,1:T(8,128)} %copy.48, bf16[768,1024]{0,1:T(8,128)(2,1)} %copy.60, f32[1024]{0:T(1024)S(1)} %copy-done.3, f32[768]{0:T(1024)S(1)} %add_rsqrt_fusion, f32[768]{0:T(1024)S(1)} %broadcast_multiply_fusion, f32[768]{0:T(1024)S(1)} %fusion.29), kind=kLoop, calls=%fused_computation.16 | loop fusion | flops 5505024 | bytes 6304768 | tf_op jit(solution)/shard_map/convert_element_type | solution.py:93
  199.9 0.0 copy-done
  199.9 0.0 copy-done.4
  199.9 0.0 copy-start.9
  199.9 0.0 copy-start.5
  199.9 0.0 copy-start.6
  199.9 0.0 copy-start.7
  199.9 0.0 copy-start.8
  199.9 3.0 %add_convert_fusion = bf16[768,1024]{1,0:T(8,128)(2,1)} fusion(bf16[768,1024]{1,0:T(8,128)(2,1)S(1)} %copy-done.4, bf16[768,1024]{0,1:T(8,128)(2,1)S(1)} %fusion.12, bf16[1024,1024]{1,0:T(8,128)(2,1)S(1)} %copy-done), kind=kOutput, calls=%fused_computation.17 | convolution fusion | flops 1612972032 | bytes 6815744 | tf_op jit(solution)/shard_map/dot_general | solution.py:95
  203.6 0.6 dynamic_slice.30
  204.8 1.4 fusion.28
  206.2 53.4 %all-gather = bf16[16,1,1024]{2,1,0:T(2,128)(2,1)S(1)} all-gather(bf16[1,1,1024]{2,1,0:T(2,128)(2,1)S(1)} %fusion.28), channel_id=1, replica_groups=mesh['rep'=2,'seq'=16] {'seq'}, dimensions={0}, use_global_device_ids=true | all-gather | bytes 34816 | tf_op jit(solution)/shard_map/all_gather | solution.py:101
  259.6 0.0 copy-done.9
  259.6 0.1 select_reduce_fusion
  259.7 0.3 convolution_convert_fusion
  259.9 0.0 copy-done.5
  259.9 0.0 copy-done.6
  260.0 0.0 copy-done.7
  260.0 0.0 copy-done.8
  260.0 2.3 fusion.18
  (17 shorter events, 0.0 us)
Async XLA Ops:
  0.6 199.2 %copy-start = (bf16[1024,1024]{1,0:T(8,128)(2,1)S(1)}, bf16[1024,1024]{1,0:T(8,128)(2,1)}, u32[]{:S(2)}) copy-start(bf16[1024,1024]{1,0:T(8,128)(2,1)} %param.19) | copy-start | bytes 6291460
  1.6 7.5 %copy-start.10 = (s32[8,1]{0,1:T(1,128)}, s32[8,1]{0,1:T(1,128)S(1)}, u32[]{:S(2)}) copy-start(s32[8,1]{0,1:T(1,128)S(1)} %reduce-window.7) | copy-start | bytes 100
  2.4 0.5 copy-start.12
  42.0 142.6 %copy-start.13 = (s32[16]{0:T(128)S(1)}, s32[16]{0:T(128)}, u32[]{:S(2)}) copy-start(s32[16]{0:T(128)} %copy-done.12) | copy-start | bytes 196
  42.0 142.6 %copy-start.11 = (s32[8,1]{0,1:T(1,128)S(1)}, s32[8,1]{0,1:T(1,128)}, u32[]{:S(2)}) copy-start(s32[8,1]{0,1:T(1,128)} %copy-done.10) | copy-start | bytes 100
  42.0 143.3 %copy-start.1 = (s32[8]{0:T(128)S(1)}, s32[8]{0:T(128)}, u32[]{:S(2)}) copy-start(s32[8]{0:T(128)} %param.21) | copy-start | bytes 100
  42.0 38.2 %collective-permute-start = (bf16[768,2048]{0,1:T(8,128)(2,1)}, bf16[768,2048]{0,1:T(8,128)(2,1)}, u32[]{:S(2)}, u32[]{:S(2)}) collective-permute-start(bf16[768,2048]{0,1:T(8,128)(2,1)} %get-tuple-element.274), channel_id=1, source_target_pairs={{0,1},{1,2},{2,3},{3,4},{4,5},{5,6},{6,7},{7,8},{8,9},{9,10},{10,1... | collective-permute-start | bytes 9437192 | tf_op jit(solution)/shard_map/while/body/eval_jaxpr/ppermute | solution.py:12
  84.0 54.1 %collective-permute-start = (bf16[768,2048]{0,1:T(8,128)(2,1)}, bf16[768,2048]{0,1:T(8,128)(2,1)}, u32[]{:S(2)}, u32[]{:S(2)}) collective-permute-start(bf16[768,2048]{0,1:T(8,128)(2,1)} %get-tuple-element.274), channel_id=1, source_target_pairs={{0,1},{1,2},{2,3},{3,4},{4,5},{5,6},{6,7},{7,8},{8,9},{9,10},{10,1... | collective-permute-start | bytes 9437192 | tf_op jit(solution)/shard_map/while/body/eval_jaxpr/ppermute | solution.py:12
  141.9 38.9 %collective-permute-start = (bf16[768,2048]{0,1:T(8,128)(2,1)}, bf16[768,2048]{0,1:T(8,128)(2,1)}, u32[]{:S(2)}, u32[]{:S(2)}) collective-permute-start(bf16[768,2048]{0,1:T(8,128)(2,1)} %get-tuple-element.274), channel_id=1, source_target_pairs={{0,1},{1,2},{2,3},{3,4},{4,5},{5,6},{6,7},{7,8},{8,9},{9,10},{10,1... | collective-permute-start | bytes 9437192 | tf_op jit(solution)/shard_map/while/body/eval_jaxpr/ppermute | solution.py:12
  185.9 3.8 %copy-start.2 = (f32[768,8,128]{2,0,1:T(8,128)S(1)}, f32[768,8,128]{2,0,1:T(8,128)}, u32[]{:S(2)}) copy-start(f32[768,8,128]{2,0,1:T(8,128)} %get-tuple-element.178) | copy-start | bytes 9437188
  194.1 2.6 copy-start.3
  196.7 3.2 %copy-start.4 = (bf16[768,1024]{1,0:T(8,128)(2,1)S(1)}, bf16[768,1024]{1,0:T(8,128)(2,1)}, u32[]{:S(2)}) copy-start(bf16[768,1024]{1,0:T(8,128)(2,1)} %param.17) | copy-start | bytes 4718596
  199.9 59.7 %copy-start.9 = (s32[128]{0:T(128)S(1)}, s32[128]{0:T(128)}, u32[]{:S(2)}) copy-start(s32[128]{0:T(128)} %param.23) | copy-start | bytes 1540
  199.9 60.1 %copy-start.5 = (bf16[128,2048]{1,0:T(8,128)(2,1)S(1)}, bf16[128,2048]{1,0:T(8,128)(2,1)}, u32[]{:S(2)}) copy-start(bf16[128,2048]{1,0:T(8,128)(2,1)} %param.25) | copy-start | bytes 1572868
  199.9 60.1 %copy-start.6 = (bf16[2048,128]{1,0:T(8,128)(2,1)S(1)}, bf16[2048,128]{1,0:T(8,128)(2,1)}, u32[]{:S(2)}) copy-start(bf16[2048,128]{1,0:T(8,128)(2,1)} %param.24) | copy-start | bytes 1572868
  199.9 60.0 %copy-start.7 = (f32[2048]{0:T(1024)S(1)}, f32[2048]{0:T(1024)}, u32[]{:S(2)}) copy-start(f32[2048]{0:T(1024)} %param.27) | copy-start | bytes 24580
  199.9 60.0 %copy-start.8 = (f32[2048]{0:T(1024)S(1)}, f32[2048]{0:T(1024)}, u32[]{:S(2)}) copy-start(f32[2048]{0:T(1024)} %param.26) | copy-start | bytes 24580
where the time goes:
time: 263 us; the launch traced here: 262 us
  waiting for transfers between devices  98 us (37%)
  blocking collectives  53.4 us (20%)
  local copies, waits for them, and re-layouts  48 us (18%)
  starting transfers between devices  27.7 us (11%)
  matrix products  17.6 us (7%)
  other arithmetic  11.7 us (4%)
  loops' own time  3.68 us (1%)
    ppermute x3, waiting for transfers between devices, shifted(): return lax.ppermute(x, axis, pairs)  98 us
    all_gather x1, blocking collectives, body(): user_rows = lax.all_gather(final_row, 'seq', axis=0, tiled=True)  53.4 us
    ppermute x3, starting transfers between devices, shifted(): return lax.ppermute(x, axis, pairs)  27.7 us
    unnamed x33, local copies, waits for them, and re-layouts  15.8 us
    dot_general x1, matrix products, attend(): jnp.einsum('hqk,khd->qhd', weights, value_part, preferred_element_type=jn...  12.1 us
    while x3, local copies, waits for them, and re-layouts  11.4 us
    while x2, local copies, waits for them, and re-layouts, body(): lax.fori_loop(1, span_limit, next_block, (totals, own_block))  6.32 us
    slice x1, local copies, waits for them, and re-layouts, body(): projected[:, :model_width].astype(jnp.float32)  5.67 us
  transfers between devices with their start and end apart: 3, of which 3 were waited for; matrix products, arithmetic and copies ran while one was open for 1% of the time, Pallas kernels for 0%

commit v1 on v0

v1 whole, which is shorter than its diff:
```python
import functools

import jax
import jax.numpy as jnp
from jax import lax
from jax.experimental import pallas as pl
from jax.experimental.pallas import tpu as pltpu
from jax.sharding import PartitionSpec as P

HEADS = 8
MESH = pl.DeviceIdType.MESH
ONE_BACK, TWO_BACK, THREE_BACK, EVEN_OWN, OWN = range(5)


def history_kernel(
    n, row_tile, flags_ref, gain_ref, proj_ref, hist_ref, weight_ref, out_ref,
    kv, queries, gates, residual, weights, attn, local_sem, side_sem, send_sem, recv_sem,
):
    rep, me = lax.axis_index("rep"), lax.axis_index("seq")
    core = lax.rem(me, 2)
    side = lax.rem(me // 2, 2)
    rows, width = residual.shape
    size = width // HEADS
    half_scale = 0.5 * size ** (-0.5)

    def dev(shift):
        return lax.rem(me + shift + n, n)

    partner = me + 1 - 2 * core

    def load(h, part, target, sem):
        columns = pl.ds(pl.multiple_of(part * width + h * size, size), size)
        return pltpu.make_async_copy(proj_ref.at[:, columns], target, sem)

    def loads(h):
        return (
            load(h, 2, kv.at[OWN, h, 0], local_sem.at[h, 0]),
            load(h, 3, kv.at[OWN, h, 1], local_sem.at[h, 1]),
            load(h, 1, queries.at[h], local_sem.at[h, 2]),
        )

    late = (
        pltpu.make_async_copy(proj_ref.at[:, pl.ds(0, width)], gates, side_sem.at[0]),
        pltpu.make_async_copy(hist_ref, residual, side_sem.at[1]),
        pltpu.make_async_copy(weight_ref, weights, side_sem.at[2]),
    )

    @pl.loop(0, HEADS)
    def _(h):
        for copy in loads(h):
            copy.start()

    for copy in late:
        copy.start()

    barrier = pltpu.get_barrier_semaphore()

    def greet(target):
        pl.semaphore_signal(barrier, inc=1, device_id=(rep, target), device_id_type=MESH)

    greet(partner)

    @pl.when(core == 0)
    def _():
        greet(dev(-2))
        pl.semaphore_wait(barrier, 2)

    @pl.when(core == 1)
    def _():
        greet(dev(-4))

        @pl.when(side == 0)
        def _():
            greet(dev(2))

        @pl.when(side == 1)
        def _():
            greet(dev(-2))

        pl.semaphore_wait(barrier, 3)

    def push(h, source, slot, target, use):
        return pltpu.make_async_remote_copy(
            src_ref=kv.at[source, h],
            dst_ref=kv.at[slot, h],
            send_sem=send_sem.at[use, h],
            recv_sem=recv_sem.at[slot, h],
            device_id=(rep, target),
            device_id_type=MESH,
        )

    def arrived(h, slot):
        push(h, slot, slot, partner, 0).wait_recv()

    def sent(h, use):
        push(h, OWN, OWN, partner, use).wait_send()

    @pl.loop(0, HEADS)
    def _(h):
        for copy in loads(h):
            copy.wait()

        @pl.when(core == 0)
        def _():
            push(h, OWN, TWO_BACK, dev(2), 0).start()
            push(h, OWN, EVEN_OWN, partner, 2).start()

        @pl.when(core == 1)
        def _():
            push(h, OWN, THREE_BACK, dev(4), 1).start()

            @pl.when(side == 0)
            def _():
                push(h, OWN, ONE_BACK, dev(2), 0).start()

    def weigh(q, k):
        half = half_scale * lax.dot_general(
            q, k, (((1,), (1,)), ((), ())), preferred_element_type=jnp.float32
        )
        return half + half * jnp.tanh(half)

    tiles = rows // row_tile
    causal = lax.broadcasted_iota(jnp.int32, (row_tile, row_tile), 1) <= (
        lax.broadcasted_iota(jnp.int32, (row_tile, row_tile), 0)
    )

    def head_columns(h):
        return pl.ds(pl.multiple_of(h * size, size), size)

    @pl.loop(0, HEADS)
    def _(h):
        for tile in range(tiles):
            low, high = tile * row_tile, (tile + 1) * row_tile
            q = queries[h, low:high]
            edge = jnp.where(causal, weigh(q, kv[OWN, h, 0, low:high]), 0.0).astype(jnp.bfloat16)
            total = jnp.dot(edge, kv[OWN, h, 1, low:high], preferred_element_type=jnp.float32)
            if tile:
                full = weigh(q, kv[OWN, h, 0, :low]).astype(jnp.bfloat16)
                total += jnp.dot(full, kv[OWN, h, 1, :low], preferred_element_type=jnp.float32)
            attn[low:high, head_columns(h)] = total

    @pl.loop(0, HEADS + 2)
    def _(step):
        @pl.when(step < HEADS)
        def _():
            h = step

            @pl.when(core == 0)
            def _():
                arrived(h, TWO_BACK)
                push(h, TWO_BACK, TWO_BACK, partner, 3).start()

            @pl.when(core == 1)
            def _():
                arrived(h, THREE_BACK)

                @pl.when(side == 1)
                def _():
                    push(h, THREE_BACK, ONE_BACK, dev(-2), 0).start()

                push(h, THREE_BACK, THREE_BACK, partner, 2).start()

                @pl.when(side == 1)
                def _():
                    arrived(h, ONE_BACK)
                    push(h, ONE_BACK, ONE_BACK, partner, 3).start()

        @pl.when((step >= 1) & (step <= HEADS) & (core == 1) & (side == 0))
        def _():
            h = step - 1
            arrived(h, ONE_BACK)
            push(h, ONE_BACK, ONE_BACK, partner, 3).start()

        @pl.when(step >= 2)
        def _():
            h = step - 2

            @pl.when(core == 0)
            def _():
                arrived(h, ONE_BACK)
                arrived(h, THREE_BACK)

            @pl.when(core == 1)
            def _():
                arrived(h, EVEN_OWN)
                arrived(h, TWO_BACK)

            for tile in range(tiles):
                low, high = tile * row_tile, (tile + 1) * row_tile
                q = queries[h, low:high]
                total = attn[low:high, head_columns(h)]
                for back in range(3):
                    slot = lax.rem(back + 3 * core, 4)
                    w = weigh(q, kv[slot, h, 0]).astype(jnp.bfloat16)
                    part = jnp.dot(w, kv[slot, h, 1], preferred_element_type=jnp.float32)
                    total += jnp.where(flags_ref[back] > 0, part, 0.0)
                attn[low:high, head_columns(h)] = total

    for copy in late:
        copy.wait()
    valid = flags_ref[3]
    gain = gain_ref[...]
    for tile in range(tiles):
        low, high = tile * row_tile, (tile + 1) * row_tile
        ids = low + lax.broadcasted_iota(jnp.int32, (row_tile, 1), 0)
        x = jnp.where(ids < valid, attn[low:high], 0.0)
        centered = x - jnp.mean(x, axis=1, keepdims=True)
        var = jnp.mean(centered * centered, axis=1, keepdims=True)
        normed = centered * lax.rsqrt(var + 1e-06) * gain
        gated = (normed * gates[low:high].astype(jnp.float32)).astype(jnp.bfloat16)
        out = jnp.dot(gated, weights[...], preferred_element_type=jnp.float32)
        out_ref[low:high] = (out + residual[low:high].astype(jnp.float32)).astype(jnp.bfloat16)

    @pl.loop(0, HEADS)
    def _(h):
        sent(h, 2)
        sent(h, 3)

        @pl.when((core == 0) | (side == 0) | (side == 1))
        def _():
            sent(h, 0)

        @pl.when(core == 1)
        def _():
            sent(h, 1)


def history_layer(n, flags, gain, projected, history_in, out_proj):
    rows, width = history_in.shape
    size = width // HEADS
    row_tile = next(t for t in (256, 128, 64, 32, 16, rows) if rows % t == 0)
    anywhere = pl.BlockSpec(memory_space=pl.ANY)
    vmem = pl.BlockSpec(memory_space=pltpu.VMEM)
    return pl.pallas_call(
        functools.partial(history_kernel, n, row_tile),
        out_shape=jax.ShapeDtypeStruct((rows, width), jnp.bfloat16),
        in_specs=[pl.BlockSpec(memory_space=pltpu.SMEM), vmem, anywhere, anywhere, anywhere],
        out_specs=vmem,
        scratch_shapes=[
            pltpu.VMEM((5, HEADS, 2, rows, size), jnp.bfloat16),
            pltpu.VMEM((HEADS, rows, size), jnp.bfloat16),
            pltpu.VMEM((rows, width), jnp.bfloat16),
            pltpu.VMEM((rows, width), jnp.bfloat16),
            pltpu.VMEM((width, width), jnp.bfloat16),
            pltpu.VMEM((rows, width), jnp.float32),
            pltpu.SemaphoreType.DMA((HEADS, 3)),
            pltpu.SemaphoreType.DMA((3,)),
            pltpu.SemaphoreType.DMA((4, HEADS)),
            pltpu.SemaphoreType.DMA((5, HEADS)),
        ],
        compiler_params=pltpu.CompilerParams(
            collective_id=0, has_side_effects=True, vmem_limit_bytes=60 * 1024 * 1024
        ),
        name="history_layer",
    )(flags, gain, projected, history_in, out_proj)


def gather_kernel(n, row_ref, rows_ref, own_sem, send_sem, recv_sem):
    rep, me = lax.axis_index("rep"), lax.axis_index("seq")
    own = pltpu.make_async_copy(row_ref, rows_ref.at[me], own_sem)
    own.start()
    barrier = pltpu.get_barrier_semaphore()

    def copy_to(shift):
        return pltpu.make_async_remote_copy(
            src_ref=row_ref,
            dst_ref=rows_ref.at[me],
            send_sem=send_sem.at[shift],
            recv_sem=recv_sem.at[shift],
            device_id=(rep, lax.rem(me + shift, n)),
            device_id_type=MESH,
        )

    @pl.loop(1, n)
    def _(shift):
        pl.semaphore_signal(
            barrier, inc=1, device_id=(rep, lax.rem(me + shift, n)), device_id_type=MESH
        )

    pl.semaphore_wait(barrier, n - 1)

    @pl.loop(1, n)
    def _(shift):
        copy_to(shift).start()

    own.wait()

    @pl.loop(1, n)
    def _(shift):
        copy_to(shift).wait_send()
        copy_to(shift).wait_recv()


def gather_rows(n, row):
    vmem = pl.BlockSpec(memory_space=pltpu.VMEM)
    width = row.shape[1]
    return pl.pallas_call(
        functools.partial(gather_kernel, n),
        out_shape=jax.ShapeDtypeStruct((n, 1, width), row.dtype),
        in_specs=[vmem],
        out_specs=vmem,
        scratch_shapes=[
            pltpu.SemaphoreType.DMA,
            pltpu.SemaphoreType.DMA((n,)),
            pltpu.SemaphoreType.DMA((n,)),
        ],
        compiler_params=pltpu.CompilerParams(collective_id=1, has_side_effects=True),
        name="gather_rows",
    )(row)


def body(
    projected,
    history_in,
    norm_gain,
    out_proj,
    user_spans,
    user_tails,
    cand_emb,
    cand_user,
    cross_down,
    cross_up,
    cross_bias,
    score_weight,
):
    row_count, model_width = history_in.shape
    devices = lax.axis_size("seq")
    my_index = lax.axis_index("seq")
    span_limit = min(4, devices // 2)
    last_dev = jnp.cumsum(user_spans) - 1
    first_dev = last_dev - user_spans + 1
    device_ids = jnp.arange(devices, dtype=jnp.int32)
    owner_of = jnp.sum((first_dev[None, :] <= device_ids[:, None]).astype(jnp.int32), axis=1) - 1
    is_end = device_ids == last_dev[owner_of]
    valid_rows = jnp.where(is_end, user_tails[owner_of], row_count)
    before = my_index - 1 - jnp.arange(3, dtype=jnp.int32)
    same_user = (before >= 0) & (owner_of[jnp.maximum(before, 0)] == owner_of[my_index])
    same_user &= jnp.arange(1, 4) < span_limit
    valid_here = valid_rows[my_index]
    flags = jnp.concatenate([same_user.astype(jnp.int32), valid_here[None].astype(jnp.int32)])
    history_out = history_layer(
        devices, flags, norm_gain[None, :], projected, history_in, out_proj
    )
    last_row = jnp.where(is_end[my_index], valid_here - 1, 0)
    final_row = lax.dynamic_slice_in_dim(history_out, last_row, 1, 0)
    final_row = jnp.where(is_end[my_index], final_row, jnp.zeros_like(final_row))
    user_rows = gather_rows(devices, final_row.astype(jnp.float32))
    user_rows = user_rows.reshape(devices, model_width).astype(jnp.bfloat16)
    user_count = user_spans.shape[0]
    user_match = cand_user[:, None] == jnp.arange(user_count, dtype=jnp.int32)[None, :]
    cand_dev = jnp.sum(jnp.where(user_match, last_dev[None, :], 0), axis=1)
    selector = (cand_dev[:, None] == device_ids[None, :]).astype(jnp.bfloat16)
    user_part = jnp.dot(selector, user_rows, preferred_element_type=jnp.float32).astype(
        jnp.bfloat16
    )
    crossed_in = jnp.concatenate([user_part, cand_emb], axis=1)
    low_rank = jnp.dot(crossed_in, cross_down, preferred_element_type=jnp.float32).astype(
        jnp.bfloat16
    )
    up_part = jnp.dot(low_rank, cross_up, preferred_element_type=jnp.float32)
    input_float = crossed_in.astype(jnp.float32)
    crossed = input_float * (up_part + cross_bias) + input_float
    scores = jnp.sum(crossed * score_weight, axis=1)
    return (history_out, scores)


def solution(mesh):
    in_specs = (
        P(("rep", "seq"), None),
        P(("rep", "seq"), None),
        P(),
        P(),
        P("rep"),
        P("rep"),
        P(("rep", "seq"), None),
        P(("rep", "seq")),
        P(),
        P(),
        P(),
        P(),
    )
    out_specs = (P(("rep", "seq"), None), P(("rep", "seq")))
    return jax.shard_map(body, mesh=mesh, in_specs=in_specs, out_specs=out_specs, check_vma=False)
```

time: 263 us -> 114 us (0.43)
  waiting for transfers between devices: 98 us -> 0 us
  Pallas kernels: 0 us -> 96.7 us
  blocking collectives: 53.4 us -> 0 us
  local copies, waits for them, and re-layouts: 48 us -> 5.79 us
  starting transfers between devices: 27.7 us -> 0 us
  matrix products: 17.6 us -> 1.47 us
  other arithmetic: 11.7 us -> 6.46 us
  loops' own time: 3.68 us -> 0 us
    ppermute x3 -> x0, waiting for transfers between devices: 98 us -> none  [shifted(): return lax.ppermute(x, axis, pairs)]
    pallas_call x0 -> x2, Pallas kernels: none -> 96.7 us  [the longest x1 89 us: history_layer(): pl.pallas_call(functools.partial(history_kernel, n, row_tile), out_shape=...]
    all_gather x1 -> x0, blocking collectives: 53.4 us -> none  [body(): user_rows = lax.all_gather(final_row, 'seq', axis=0, tiled=True)]
    ppermute x3 -> x0, starting transfers between devices: 27.7 us -> none  [shifted(): return lax.ppermute(x, axis, pairs)]
    while x5 -> x0, local copies, waits for them, and re-layouts: 17.7 us -> none
    dot_general x2 -> x0, matrix products: 15.1 us -> none  [the longest x1 12.1 us: attend(): jnp.einsum('hqk,khd->qhd', weights, value_part, preferred_element_type=jn...]
    unnamed x33 -> x15, local copies, waits for them, and re-layouts: 15.8 us -> 1.37 us
    slice x2 -> x0, local copies, waits for them, and re-layouts: 9.63 us -> none  [the longest x1 5.67 us: body(): projected[:, :model_width].astype(jnp.float32)]
  transfers between devices with their start and end apart: 3 -> 0, of which waited for: 3 -> 0; matrix products, arithmetic and copies ran while one was open for 1% -> 0% of each run, Pallas kernels for 0% -> 0%
where the time goes in v1:
time: 114 us; the launch traced here: 112 us
  Pallas kernels  96.7 us (85%)
  other arithmetic  6.46 us (6%)
  local copies, waits for them, and re-layouts  5.79 us (5%)
  between operations  2.04 us (2%)
  matrix products  1.47 us (1%)
    pallas_call x1, Pallas kernels, history_layer(): pl.pallas_call(functools.partial(history_kernel, n, row_tile), out_shape=...  89 us
    pallas_call x1, Pallas kernels, gather_rows(): pl.pallas_call(functools.partial(gather_kernel, n), out_shape=jax.ShapeDt...  7.7 us

profile of v1, /device:TPU:3, one launch (start us, length us, event | category | flops | bytes accessed | tf_op | source)
XLA Modules:
  0.0 112.4 jit_solution(13546381063164778488)
XLA Ops:
  0.6 0.0 copy-start
  0.6 0.9 reduce-window.7
  1.5 0.7 subtract_add_fusion
  2.2 0.1 convert_reduce_fusion
  2.3 0.7 gather_fusion.1
  3.0 1.3 %gather_fusion.2 = s32[16]{0:T(128)S(1)} fusion(s32[8]{0:T(128)} %param.17, s32[1024]{0:T(1024)S(1)} %pad_clamp_fusion), kind=kCustom, calls=%fused_computation.2 | custom fusion | bytes 192 | tf_op jit(solution)/shard_map/gather | solution.py:335
  4.3 0.6 dynamic_slice.14
  5.6 0.6 dynamic_slice.15
  6.8 0.6 dynamic_slice.13
  7.4 0.6 gather_fusion
  8.0 0.7 and_convert_fusion
  8.7 1.2 %pad_add_fusion.flags_ref = s32[4]{0:T(128)} fusion(s32[1]{0:T(128)} %dynamic_slice.14, s32[3]{0:T(128)S(1)} %and_convert_fusion), kind=kLoop, calls=%fused_computation.28 | loop fusion | flops 4 | bytes 32 | tf_op jit(solution)/shard_map/concatenate | solution.py:340
  9.9 0.0 copy-start.6
  9.9 0.0 copy-start.2
  9.9 0.0 copy-start.3
  9.9 0.0 copy-start.4
  9.9 0.0 copy-start.5
  10.0 89.0 %history_layer.1 = bf16[768,1024]{1,0:T(8,128)(2,1)} custom-call(s32[4]{0:T(128)} %pad_add_fusion.flags_ref, f32[1,1024]{1,0:T(1,128)} %bitcast.22, bf16[768,4096]{1,0:T(8,128)(2,1)} %proj_ref.1, bf16[768,1024]{1,0:T(8,128)(2,1)} %hist_ref.1, bf16[1024,1024]{1,0:T(8,128)(2,1)} %weight_ref.1), custom_call_target="tpu_custom_call" | custom-call | tf_op jit(solution)/shard_map/history_layer/pallas_call | solution.py:234
  98.9 1.9 %fusion.13.row_ref = f32[1,1024]{1,0:T(1,128)} fusion(pred[]{:T(512)} %bitcast.8, bf16[768,1024]{1,0:T(8,128)(2,1)} %history_layer.1, s32[]{:T(128)S(6)} %select_n.47), kind=kLoop, calls=%fused_computation.18 | loop fusion | flops 2048 | bytes 6149 | tf_op jit(solution)/shard_map/convert_element_type | solution.py:347
  100.9 7.7 %gather_rows.1 = f32[16,1,1024]{2,1,0:T(1,128)} custom-call(f32[1,1024]{1,0:T(1,128)} %fusion.13.row_ref), custom_call_target="tpu_custom_call" | custom-call | tf_op jit(solution)/shard_map/gather_rows/pallas_call | solution.py:297
  108.6 0.9 convert_element_type.28
  109.5 0.0 copy-done.6
  109.5 0.1 select_reduce_fusion
  109.6 0.3 convolution_convert_fusion
  109.8 0.0 copy-done
  109.8 0.0 copy-done.2
  109.8 0.0 copy-done.3
  109.9 0.0 copy-done.4
  109.9 0.0 copy-done.5
  109.9 0.0 copy-start.1
  109.9 1.2 %fusion.3 = f32[128]{0:T(128)} fusion(bf16[128,2048]{1,0:T(8,128)(2,1)S(1)} %copy-done, bf16[2048,128]{1,0:T(8,128)(2,1)S(1)} %copy-done.2, bf16[128,1024]{1,0:T(8,128)(2,1)S(1)} %copy-done.3, bf16[128,1024]{1,0:T(8,128)(2,1)S(1)} %convolution_convert_fusion, f32[2048]{0:T(1024)S(1)} %copy-done.4, f32[2048]{0:T(1024)S(1)} %copy-done.5), kind=kOutput, calls=%fused_computation.7 | convolution fusion | flops 137641856 | bytes 1589760 | tf_op jit(solution)/shard_map/dot_general | solution.py:360
  111.1 0.2 copy-done.1
  111.3 1.1 %copy.20 = bf16[768,1024]{1,0:T(8,128)(2,1)} copy(bf16[768,1024]{1,0:T(8,128)(2,1)S(1)} %copy-done.1) | data formatting | bytes 3145728
  (8 shorter events, 0.0 us)
Async XLA Ops:
  0.6 109.2 %copy-start = (bf16[128,2048]{1,0:T(8,128)(2,1)S(1)}, bf16[128,2048]{1,0:T(8,128)(2,1)}, u32[]{:S(2)}) copy-start(bf16[128,2048]{1,0:T(8,128)(2,1)} %param.21) | copy-start | bytes 1572868
  9.9 99.5 %copy-start.6 = (s32[128]{0:T(128)S(1)}, s32[128]{0:T(128)}, u32[]{:S(2)}) copy-start(s32[128]{0:T(128)} %param.19) | copy-start | bytes 1540
  9.9 99.9 %copy-start.2 = (bf16[2048,128]{1,0:T(8,128)(2,1)S(1)}, bf16[2048,128]{1,0:T(8,128)(2,1)}, u32[]{:S(2)}) copy-start(bf16[2048,128]{1,0:T(8,128)(2,1)} %param.20) | copy-start | bytes 1572868
  9.9 99.9 %copy-start.3 = (bf16[128,1024]{1,0:T(8,128)(2,1)S(1)}, bf16[128,1024]{1,0:T(8,128)(2,1)}, u32[]{:S(2)}) copy-start(bf16[128,1024]{1,0:T(8,128)(2,1)} %param.18) | copy-start | bytes 786436
  9.9 99.9 %copy-start.4 = (f32[2048]{0:T(1024)S(1)}, f32[2048]{0:T(1024)}, u32[]{:S(2)}) copy-start(f32[2048]{0:T(1024)} %param.23) | copy-start | bytes 24580
  9.9 99.9 %copy-start.5 = (f32[2048]{0:T(1024)S(1)}, f32[2048]{0:T(1024)}, u32[]{:S(2)}) copy-start(f32[2048]{0:T(1024)} %param.22) | copy-start | bytes 24580
  109.9 1.4 %copy-start.1 = (bf16[768,1024]{1,0:T(8,128)(2,1)S(1)}, bf16[768,1024]{1,0:T(8,128)(2,1)}, u32[]{:S(2)}) copy-start(bf16[768,1024]{1,0:T(8,128)(2,1)} %history_layer.1) | copy-start | bytes 4718596

commit v2 on v1

v2 whole, which is shorter than its diff:
```python
import functools

import jax
import jax.numpy as jnp
from jax import lax
from jax.experimental import pallas as pl
from jax.experimental.pallas import tpu as pltpu
from jax.sharding import PartitionSpec as P

HEADS = 8
MESH = pl.DeviceIdType.MESH
ONE_BACK, TWO_BACK, THREE_BACK, EVEN_OWN, OWN = range(5)


def history_kernel(
    n, row_tile, spans_ref, tails_ref, gain_ref, proj_ref, hist_ref, weight_ref, out_ref, rows_ref,
    kv, queries, gates, residual, weights, attn, final_row,
    local_sem, side_sem, send_sem, recv_sem, row_send_sem, row_recv_sem,
):
    rep, me = lax.axis_index("rep"), lax.axis_index("seq")
    core = lax.rem(me, 2)
    side = lax.rem(me // 2, 2)
    rows, width = residual.shape
    size = width // HEADS
    half_scale = 0.5 * size ** (-0.5)

    def dev(shift):
        return lax.rem(me + shift + n, n)

    partner = me + 1 - 2 * core

    def load(h, part, target, sem):
        columns = pl.ds(pl.multiple_of(part * width + h * size, size), size)
        return pltpu.make_async_copy(proj_ref.at[:, columns], target, sem)

    def loads(h):
        return (
            load(h, 2, kv.at[OWN, h, 0], local_sem.at[h, 0]),
            load(h, 3, kv.at[OWN, h, 1], local_sem.at[h, 1]),
            load(h, 1, queries.at[h], local_sem.at[h, 2]),
        )

    late = (
        pltpu.make_async_copy(proj_ref.at[:, pl.ds(0, width)], gates, side_sem.at[0]),
        pltpu.make_async_copy(hist_ref, residual, side_sem.at[1]),
        pltpu.make_async_copy(weight_ref, weights, side_sem.at[2]),
    )

    @pl.loop(0, HEADS)
    def _(h):
        for copy in loads(h):
            copy.start()

    for copy in late:
        copy.start()

    barrier = pltpu.get_barrier_semaphore()

    @pl.loop(1, n)
    def _(shift):
        pl.semaphore_signal(
            barrier, inc=1, device_id=(rep, dev(shift)), device_id_type=MESH
        )

    def scan_user(user, found):
        start, first, last, tail = found
        end = start + spans_ref[user]
        mine = (start <= me) & (me < end)
        return (
            end,
            jnp.where(mine, start, first),
            jnp.where(mine, end - 1, last),
            jnp.where(mine, tails_ref[user], tail),
        )

    zero = jnp.int32(0)
    _, first, last, tail = lax.fori_loop(
        0, spans_ref.shape[0], scan_user, (zero, zero, zero, zero)
    )
    valid = jnp.where(me == last, tail, rows)

    pl.semaphore_wait(barrier, n - 1)

    def push(h, source, slot, target, use):
        return pltpu.make_async_remote_copy(
            src_ref=kv.at[source, h],
            dst_ref=kv.at[slot, h],
            send_sem=send_sem.at[use, h],
            recv_sem=recv_sem.at[slot, h],
            device_id=(rep, target),
            device_id_type=MESH,
        )

    def arrived(h, slot):
        push(h, slot, slot, partner, 0).wait_recv()

    def sent(h, use):
        push(h, OWN, OWN, partner, use).wait_send()

    @pl.loop(0, HEADS)
    def _(h):
        for copy in loads(h):
            copy.wait()

        @pl.when(core == 0)
        def _():
            push(h, OWN, TWO_BACK, dev(2), 0).start()
            push(h, OWN, EVEN_OWN, partner, 2).start()

        @pl.when(core == 1)
        def _():
            push(h, OWN, THREE_BACK, dev(4), 1).start()

            @pl.when(side == 0)
            def _():
                push(h, OWN, ONE_BACK, dev(2), 0).start()

    def weigh(q, k):
        half = half_scale * lax.dot_general(
            q, k, (((1,), (1,)), ((), ())), preferred_element_type=jnp.float32
        )
        return half + half * jnp.tanh(half)

    tiles = rows // row_tile
    causal = lax.broadcasted_iota(jnp.int32, (row_tile, row_tile), 1) <= (
        lax.broadcasted_iota(jnp.int32, (row_tile, row_tile), 0)
    )

    def head_columns(h):
        return pl.ds(pl.multiple_of(h * size, size), size)

    @pl.loop(0, HEADS)
    def _(h):
        for tile in range(tiles):
            low, high = tile * row_tile, (tile + 1) * row_tile
            q = queries[h, low:high]
            edge = jnp.where(causal, weigh(q, kv[OWN, h, 0, low:high]), 0.0).astype(jnp.bfloat16)
            total = jnp.dot(edge, kv[OWN, h, 1, low:high], preferred_element_type=jnp.float32)
            if tile:
                full = weigh(q, kv[OWN, h, 0, :low]).astype(jnp.bfloat16)
                total += jnp.dot(full, kv[OWN, h, 1, :low], preferred_element_type=jnp.float32)
            attn[low:high, head_columns(h)] = total

    def absorb(h, blocks):
        for tile in range(tiles):
            low, high = tile * row_tile, (tile + 1) * row_tile
            q = queries[h, low:high]
            total = attn[low:high, head_columns(h)]
            for slot, back in blocks:
                w = weigh(q, kv[slot, h, 0]).astype(jnp.bfloat16)
                part = jnp.dot(w, kv[slot, h, 1], preferred_element_type=jnp.float32)
                total += jnp.where(me - back >= first, part, 0.0)
            attn[low:high, head_columns(h)] = total

    @pl.loop(0, HEADS + 1)
    def _(step):
        @pl.when(step < HEADS)
        def _():
            h = step

            @pl.when(core == 0)
            def _():
                arrived(h, TWO_BACK)
                push(h, TWO_BACK, TWO_BACK, partner, 3).start()

            @pl.when(core == 1)
            def _():
                arrived(h, EVEN_OWN)
                absorb(h, ((EVEN_OWN, 1),))
                arrived(h, THREE_BACK)

                @pl.when(side == 1)
                def _():
                    push(h, THREE_BACK, ONE_BACK, dev(-2), 0).start()

                push(h, THREE_BACK, THREE_BACK, partner, 2).start()

                @pl.when(side == 1)
                def _():
                    arrived(h, ONE_BACK)
                    push(h, ONE_BACK, ONE_BACK, partner, 3).start()

        @pl.when(step >= 1)
        def _():
            h = step - 1

            @pl.when(core == 0)
            def _():
                arrived(h, ONE_BACK)
                arrived(h, THREE_BACK)
                absorb(h, ((ONE_BACK, 1), (TWO_BACK, 2), (THREE_BACK, 3)))

            @pl.when(core == 1)
            def _():
                @pl.when(side == 0)
                def _():
                    arrived(h, ONE_BACK)
                    push(h, ONE_BACK, ONE_BACK, partner, 3).start()

                arrived(h, TWO_BACK)
                absorb(h, ((ONE_BACK, 2), (TWO_BACK, 3)))

    for copy in late:
        copy.wait()
    gain = gain_ref[...]

    def finish(x, gate, rest):
        centered = x - jnp.mean(x, axis=1, keepdims=True)
        var = jnp.mean(centered * centered, axis=1, keepdims=True)
        normed = centered * lax.rsqrt(var + 1e-06) * gain
        gated = (normed * gate.astype(jnp.float32)).astype(jnp.bfloat16)
        out = jnp.dot(gated, weights[...], preferred_element_type=jnp.float32)
        return (out + rest.astype(jnp.float32)).astype(jnp.bfloat16)

    final = jnp.clip(valid - 1, 0, rows - 1)
    at_last = lax.broadcasted_iota(jnp.int32, (16, rows), 1) == final
    pick = jnp.where(at_last, 1.0, 0.0).astype(jnp.bfloat16)
    picked = finish(
        jnp.broadcast_to(attn[pl.ds(final, 1), :], (16, width)),
        jnp.dot(pick, gates[...], preferred_element_type=jnp.float32),
        jnp.dot(pick, residual[...], preferred_element_type=jnp.float32),
    ).astype(jnp.float32)[0:1]
    final_row[...] = picked
    rows_ref[me] = picked

    def row_to(shift):
        return pltpu.make_async_remote_copy(
            src_ref=final_row,
            dst_ref=rows_ref.at[me],
            send_sem=row_send_sem.at[shift],
            recv_sem=row_recv_sem.at[shift],
            device_id=(rep, dev(shift)),
            device_id_type=MESH,
        )

    for tile in range(tiles):
        low, high = tile * row_tile, (tile + 1) * row_tile
        ids = low + lax.broadcasted_iota(jnp.int32, (row_tile, 1), 0)
        x = jnp.where(ids < valid, attn[low:high], 0.0)
        out_ref[low:high] = finish(x, gates[low:high], residual[low:high])
        if tile == 0:

            @pl.loop(1, n)
            def _(shift):
                row_to(shift).start()

    @pl.loop(1, n)
    def _(shift):
        row_to(shift).wait_send()
        row_to(shift).wait_recv()

    @pl.loop(0, HEADS)
    def _(h):
        sent(h, 2)
        sent(h, 3)
        sent(h, 0)

        @pl.when(core == 1)
        def _():
            sent(h, 1)


def history_layer(n, spans, tails, gain, projected, history_in, out_proj):
    rows, width = history_in.shape
    size = width // HEADS
    row_tile = next(t for t in (256, 128, 64, 32, 16, rows) if rows % t == 0)
    smem = pl.BlockSpec(memory_space=pltpu.SMEM)
    anywhere = pl.BlockSpec(memory_space=pl.ANY)
    vmem = pl.BlockSpec(memory_space=pltpu.VMEM)
    return pl.pallas_call(
        functools.partial(history_kernel, n, row_tile),
        out_shape=(
            jax.ShapeDtypeStruct((rows, width), jnp.bfloat16),
            jax.ShapeDtypeStruct((n, 1, width), jnp.float32),
        ),
        in_specs=[smem, smem, vmem, anywhere, anywhere, anywhere],
        out_specs=(vmem, vmem),
        scratch_shapes=[
            pltpu.VMEM((5, HEADS, 2, rows, size), jnp.bfloat16),
            pltpu.VMEM((HEADS, rows, size), jnp.bfloat16),
            pltpu.VMEM((rows, width), jnp.bfloat16),
            pltpu.VMEM((rows, width), jnp.bfloat16),
            pltpu.VMEM((width, width), jnp.bfloat16),
            pltpu.VMEM((rows, width), jnp.float32),
            pltpu.VMEM((1, width), jnp.float32),
            pltpu.SemaphoreType.DMA((HEADS, 3)),
            pltpu.SemaphoreType.DMA((3,)),
            pltpu.SemaphoreType.DMA((4, HEADS)),
            pltpu.SemaphoreType.DMA((5, HEADS)),
            pltpu.SemaphoreType.DMA((n,)),
            pltpu.SemaphoreType.DMA((n,)),
        ],
        compiler_params=pltpu.CompilerParams(
            collective_id=0, has_side_effects=True, vmem_limit_bytes=60 * 1024 * 1024
        ),
        name="history_layer",
    )(spans, tails, gain, projected, history_in, out_proj)


def body(
    projected,
    history_in,
    norm_gain,
    out_proj,
    user_spans,
    user_tails,
    cand_emb,
    cand_user,
    cross_down,
    cross_up,
    cross_bias,
    score_weight,
):
    model_width = history_in.shape[1]
    devices = lax.axis_size("seq")
    history_out, user_rows = history_layer(
        devices, user_spans, user_tails, norm_gain[None, :], projected, history_in, out_proj
    )
    user_rows = user_rows.reshape(devices, model_width).astype(jnp.bfloat16)
    device_ids = jnp.arange(devices, dtype=jnp.int32)
    user_count = user_spans.shape[0]
    users = jnp.arange(user_count, dtype=jnp.int32)
    last_dev = jnp.sum(jnp.where(users[None, :] <= users[:, None], user_spans[None, :], 0), axis=1) - 1
    user_match = cand_user[:, None] == jnp.arange(user_count, dtype=jnp.int32)[None, :]
    cand_dev = jnp.sum(jnp.where(user_match, last_dev[None, :], 0), axis=1)
    selector = (cand_dev[:, None] == device_ids[None, :]).astype(jnp.bfloat16)
    user_part = jnp.dot(selector, user_rows, preferred_element_type=jnp.float32).astype(
        jnp.bfloat16
    )
    crossed_in = jnp.concatenate([user_part, cand_emb], axis=1)
    low_rank = jnp.dot(crossed_in, cross_down, preferred_element_type=jnp.float32).astype(
        jnp.bfloat16
    )
    up_part = jnp.dot(low_rank, cross_up, preferred_element_type=jnp.float32)
    input_float = crossed_in.astype(jnp.float32)
    crossed = input_float * (up_part + cross_bias) + input_float
    scores = jnp.sum(crossed * score_weight, axis=1)
    return (history_out, scores)


def solution(mesh):
    in_specs = (
        P(("rep", "seq"), None),
        P(("rep", "seq"), None),
        P(),
        P(),
        P("rep"),
        P("rep"),
        P(("rep", "seq"), None),
        P(("rep", "seq")),
        P(),
        P(),
        P(),
        P(),
    )
    out_specs = (P(("rep", "seq"), None), P(("rep", "seq")))
    return jax.shard_map(body, mesh=mesh, in_specs=in_specs, out_specs=out_specs, check_vma=False)
```

time: 114 us -> 97.1 us (0.85)
  Pallas kernels: 96.7 us -> 91.1 us
  other arithmetic: 6.46 us -> 1.09 us
  local copies, waits for them, and re-layouts: 5.79 us -> 1.37 us
  between operations: 2.04 us -> 0.77 us
    pallas_call x1 -> x0, Pallas kernels: 7.7 us -> none  [gather_rows(): pl.pallas_call(functools.partial(gather_kernel, n), out_shape=jax.ShapeDt...]
    gather x3 -> x0, local copies, waits for them, and re-layouts: 2.62 us -> none  [the longest x1 1.32 us: body(): valid_rows = jnp.where(is_end, user_tails[owner_of], row_count)]
    convert_element_type x2 -> x0, other arithmetic: 2.58 us -> none  [the longest x1 1.92 us: body(): user_rows = gather_rows(devices, final_row.astype(jnp.float32))]
    pallas_call x1, Pallas kernels: 89 us -> 91.1 us  [history_layer(): pl.pallas_call(functools.partial(history_kernel, n, row_tile), out_shape=...]
    dynamic_slice x3 -> x0, local copies, waits for them, and re-layouts: 1.8 us -> none  [the longest x1 0.62 us: body(): is_end[my_index]]
    concatenate x1 -> x0, other arithmetic: 1.23 us -> none  [body(): jnp.concatenate([same_user.astype(jnp.int32), valid_here[None].astype(jnp...]
where the time goes in v2:
time: 97.1 us; the launch traced here: 95.8 us
  Pallas kernels  91.1 us (94%)
  matrix products  1.48 us (2%)
  local copies, waits for them, and re-layouts  1.37 us (1%)
  other arithmetic  1.09 us (1%)
    pallas_call x1, Pallas kernels, history_layer(): pl.pallas_call(functools.partial(history_kernel, n, row_tile), out_shape=...  91.1 us

profile of v2, /device:TPU:3, one launch (start us, length us, event | category | flops | bytes accessed | tf_op | source)
XLA Modules:
  0.0 95.8 jit_solution(17915895695200543804)
XLA Ops:
  0.6 0.0 copy-start
  0.6 0.0 copy-start.2
  0.7 0.0 copy-start.7
  0.7 0.0 copy-start.3
  0.7 0.0 copy-start.4
  0.7 0.0 copy-start.5
  0.7 0.0 copy-start.6
  0.7 91.1 %history_layer.1 = (bf16[768,1024]{1,0:T(8,128)(2,1)}, f32[16,1,1024]{2,1,0:T(1,128)}) custom-call(s32[8]{0:T(128)} %spans_ref.1, s32[8]{0:T(128)} %tails_ref.1, f32[1,1024]{1,0:T(1,128)} %bitcast.6, bf16[768,4096]{1,0:T(8,128)(2,1)} %proj_ref.1, bf16[768,1024]{1,0:T(8,128)(2,1)} %hist_ref.1, bf16[1024,1024]{1,0:T(8,128)(2,1)} %weight_ref.1), custom_call_target="tpu_custom_call" | custom-call | tf_op jit(solution)/shard_map/history_layer/pallas_call | solution.py:270
  91.8 0.9 convert_element_type.16
  92.7 0.0 copy-done.2
  92.7 0.1 select_reduce_fusion.1
  92.8 0.0 copy-done.7
  92.8 0.1 select_reduce_fusion
  92.9 0.3 convolution_convert_fusion
  93.2 0.0 copy-done
  93.2 0.0 copy-done.3
  93.2 0.0 copy-done.4
  93.2 0.0 copy-done.5
  93.2 0.0 copy-done.6
  93.3 0.0 copy-start.1
  93.3 1.2 %fusion.3 = f32[128]{0:T(128)} fusion(bf16[128,2048]{1,0:T(8,128)(2,1)S(1)} %copy-done, bf16[2048,128]{1,0:T(8,128)(2,1)S(1)} %copy-done.3, bf16[128,1024]{1,0:T(8,128)(2,1)S(1)} %copy-done.4, bf16[128,1024]{1,0:T(8,128)(2,1)S(1)} %convolution_convert_fusion, f32[2048]{0:T(1024)S(1)} %copy-done.5, f32[2048]{0:T(1024)S(1)} %copy-done.6), kind=kOutput, calls=%fused_computation.4 | convolution fusion | flops 137641856 | bytes 1589760 | tf_op jit(solution)/shard_map/dot_general | solution.py:334
  94.5 0.2 copy-done.1
  94.7 1.1 %copy.20 = bf16[768,1024]{1,0:T(8,128)(2,1)} copy(bf16[768,1024]{1,0:T(8,128)(2,1)S(1)} %copy-done.1) | data formatting | bytes 3145728
  (1 shorter events, 0.0 us)
Async XLA Ops:
  0.6 92.6 %copy-start = (bf16[128,2048]{1,0:T(8,128)(2,1)S(1)}, bf16[128,2048]{1,0:T(8,128)(2,1)}, u32[]{:S(2)}) copy-start(bf16[128,2048]{1,0:T(8,128)(2,1)} %param.21) | copy-start | bytes 1572868
  0.6 92.1 %copy-start.2 = (s32[8]{0:T(128)S(1)}, s32[8]{0:T(128)}, u32[]{:S(2)}) copy-start(s32[8]{0:T(128)} %spans_ref.1) | copy-start | bytes 100
  0.7 92.2 %copy-start.7 = (s32[128]{0:T(128)S(1)}, s32[128]{0:T(128)}, u32[]{:S(2)}) copy-start(s32[128]{0:T(128)} %param.19) | copy-start | bytes 1540
  0.7 92.5 %copy-start.3 = (bf16[2048,128]{1,0:T(8,128)(2,1)S(1)}, bf16[2048,128]{1,0:T(8,128)(2,1)}, u32[]{:S(2)}) copy-start(bf16[2048,128]{1,0:T(8,128)(2,1)} %param.20) | copy-start | bytes 1572868
  0.7 92.5 %copy-start.4 = (bf16[128,1024]{1,0:T(8,128)(2,1)S(1)}, bf16[128,1024]{1,0:T(8,128)(2,1)}, u32[]{:S(2)}) copy-start(bf16[128,1024]{1,0:T(8,128)(2,1)} %param.18) | copy-start | bytes 786436
  0.7 92.5 %copy-start.5 = (f32[2048]{0:T(1024)S(1)}, f32[2048]{0:T(1024)}, u32[]{:S(2)}) copy-start(f32[2048]{0:T(1024)} %param.23) | copy-start | bytes 24580
  0.7 92.5 %copy-start.6 = (f32[2048]{0:T(1024)S(1)}, f32[2048]{0:T(1024)}, u32[]{:S(2)}) copy-start(f32[2048]{0:T(1024)} %param.22) | copy-start | bytes 24580
  93.3 1.4 %copy-start.1 = (bf16[768,1024]{1,0:T(8,128)(2,1)S(1)}, bf16[768,1024]{1,0:T(8,128)(2,1)}, u32[]{:S(2)}) copy-start(bf16[768,1024]{1,0:T(8,128)(2,1)} %get-tuple-element.8) | copy-start | bytes 4718596

commit v3 on v2

--- a/solution.py
+++ b/solution.py
@@ -13,8 +13,8 @@
 
 
 def history_kernel(
-    n, row_tile, spans_ref, tails_ref, gain_ref, proj_ref, hist_ref, weight_ref, out_ref, rows_ref,
-    kv, queries, gates, residual, weights, attn, final_row,
+    n, row_tile, spans_ref, tails_ref, gain_ref, proj_ref, hist_ref, weight_ref, out_ref, table_ref,
+    kv, queries, gates, residual, weights, attn, final_row, rows_ref,
     local_sem, side_sem, send_sem, recv_sem, row_send_sem, row_recv_sem,
 ):
     rep, me = lax.axis_index("rep"), lax.axis_index("seq")
@@ -249,6 +249,10 @@
         row_to(shift).wait_send()
         row_to(shift).wait_recv()
 
+    @pl.loop(0, n)
+    def _(index):
+        table_ref[pl.ds(index, 1), :] = rows_ref[index]
+
     @pl.loop(0, HEADS)
     def _(h):
         sent(h, 2)
@@ -271,7 +275,7 @@
         functools.partial(history_kernel, n, row_tile),
         out_shape=(
             jax.ShapeDtypeStruct((rows, width), jnp.bfloat16),
-            jax.ShapeDtypeStruct((n, 1, width), jnp.float32),
+            jax.ShapeDtypeStruct((n, width), jnp.float32),
         ),
         in_specs=[smem, smem, vmem, anywhere, anywhere, anywhere],
         out_specs=(vmem, vmem),
@@ -283,6 +287,7 @@
             pltpu.VMEM((width, width), jnp.bfloat16),
             pltpu.VMEM((rows, width), jnp.float32),
             pltpu.VMEM((1, width), jnp.float32),
+            pltpu.VMEM((n, 1, width), jnp.float32),
             pltpu.SemaphoreType.DMA((HEADS, 3)),
             pltpu.SemaphoreType.DMA((3,)),
             pltpu.SemaphoreType.DMA((4, HEADS)),
@@ -311,12 +316,11 @@
     cross_bias,
     score_weight,
 ):
-    model_width = history_in.shape[1]
     devices = lax.axis_size("seq")
     history_out, user_rows = history_layer(
         devices, user_spans, user_tails, norm_gain[None, :], projected, history_in, out_proj
     )
-    user_rows = user_rows.reshape(devices, model_width).astype(jnp.bfloat16)
+    user_rows = user_rows.astype(jnp.bfloat16)
     device_ids = jnp.arange(devices, dtype=jnp.int32)
     user_count = user_spans.shape[0]
     users = jnp.arange(user_count, dtype=jnp.int32)

time: 97.1 us -> 97.2 us (level)
  no operation moved by 1% of the time
where the time goes in v3:
time: 97.2 us; the launch traced here: 95.9 us
  Pallas kernels  91.2 us (94%)
  matrix products  2.32 us (2%)
  local copies, waits for them, and re-layouts  1.36 us (1%)
    pallas_call x1, Pallas kernels, history_layer(): pl.pallas_call(functools.partial(history_kernel, n, row_tile), out_shape=...  91.2 us

profile of v3, /device:TPU:3, one launch (start us, length us, event | category | flops | bytes accessed | tf_op | source)
XLA Modules:
  0.0 95.9 jit_solution(12556210255116313629)
XLA Ops:
  0.6 0.0 copy-start
  0.6 0.0 copy-start.2
  0.7 0.0 copy-start.7
  0.7 0.0 copy-start.3
  0.7 0.0 copy-start.4
  0.7 0.0 copy-start.5
  0.7 0.0 copy-start.6
  0.7 91.2 %history_layer.1 = (bf16[768,1024]{1,0:T(8,128)(2,1)}, f32[16,1024]{1,0:T(8,128)}) custom-call(s32[8]{0:T(128)} %spans_ref.1, s32[8]{0:T(128)} %tails_ref.1, f32[1,1024]{1,0:T(1,128)} %bitcast.3, bf16[768,4096]{1,0:T(8,128)(2,1)} %proj_ref.1, bf16[768,1024]{1,0:T(8,128)(2,1)} %hist_ref.1, bf16[1024,1024]{1,0:T(8,128)(2,1)} %weight_ref.1), custom_call_target="tpu_custom_call" | custom-call | tf_op jit(solution)/shard_map/history_layer/pallas_call | solution.py:274
  91.9 0.0 copy-done.2
  91.9 0.1 select_reduce_fusion.1
  92.1 0.0 copy-done.7
  92.1 0.1 select_reduce_fusion
  92.1 1.1 %convolution_convert_fusion = bf16[128,1024]{1,0:T(8,128)(2,1)S(1)} fusion(f32[16,1024]{1,0:T(8,128)} %get-tuple-element.5, s32[128]{0:T(128)S(1)} %select_reduce_fusion), kind=kOutput, calls=%fused_computation.5 | convolution fusion | flops 4343808 | bytes 328192 | tf_op jit(solution)/shard_map/dot_general | solution.py:331
  93.3 0.0 copy-done
  93.3 0.0 copy-done.3
  93.3 0.0 copy-done.4
  93.3 0.0 copy-done.5
  93.3 0.0 copy-done.6
  93.3 0.0 copy-start.1
  93.3 1.2 %fusion.3 = f32[128]{0:T(128)} fusion(bf16[128,2048]{1,0:T(8,128)(2,1)S(1)} %copy-done, bf16[2048,128]{1,0:T(8,128)(2,1)S(1)} %copy-done.3, bf16[128,1024]{1,0:T(8,128)(2,1)S(1)} %copy-done.4, bf16[128,1024]{1,0:T(8,128)(2,1)S(1)} %convolution_convert_fusion, f32[2048]{0:T(1024)S(1)} %copy-done.5, f32[2048]{0:T(1024)S(1)} %copy-done.6), kind=kOutput, calls=%fused_computation.4 | convolution fusion | flops 137641856 | bytes 1589760 | tf_op jit(solution)/shard_map/dot_general | solution.py:338
  94.5 0.2 copy-done.1
  94.7 1.1 %copy.15 = bf16[768,1024]{1,0:T(8,128)(2,1)} copy(bf16[768,1024]{1,0:T(8,128)(2,1)S(1)} %copy-done.1) | data formatting | bytes 3145728
  (1 shorter events, 0.0 us)
Async XLA Ops:
  0.6 92.6 %copy-start = (bf16[128,2048]{1,0:T(8,128)(2,1)S(1)}, bf16[128,2048]{1,0:T(8,128)(2,1)}, u32[]{:S(2)}) copy-start(bf16[128,2048]{1,0:T(8,128)(2,1)} %param.21) | copy-start | bytes 1572868
  0.6 91.3 %copy-start.2 = (s32[8]{0:T(128)S(1)}, s32[8]{0:T(128)}, u32[]{:S(2)}) copy-start(s32[8]{0:T(128)} %spans_ref.1) | copy-start | bytes 100
  0.7 91.4 %copy-start.7 = (s32[128]{0:T(128)S(1)}, s32[128]{0:T(128)}, u32[]{:S(2)}) copy-start(s32[128]{0:T(128)} %param.19) | copy-start | bytes 1540
  0.7 92.6 %copy-start.3 = (bf16[2048,128]{1,0:T(8,128)(2,1)S(1)}, bf16[2048,128]{1,0:T(8,128)(2,1)}, u32[]{:S(2)}) copy-start(bf16[2048,128]{1,0:T(8,128)(2,1)} %param.20) | copy-start | bytes 1572868
  0.7 92.6 %copy-start.4 = (bf16[128,1024]{1,0:T(8,128)(2,1)S(1)}, bf16[128,1024]{1,0:T(8,128)(2,1)}, u32[]{:S(2)}) copy-start(bf16[128,1024]{1,0:T(8,128)(2,1)} %param.18) | copy-start | bytes 786436
  0.7 92.6 %copy-start.5 = (f32[2048]{0:T(1024)S(1)}, f32[2048]{0:T(1024)}, u32[]{:S(2)}) copy-start(f32[2048]{0:T(1024)} %param.23) | copy-start | bytes 24580
  0.7 92.6 %copy-start.6 = (f32[2048]{0:T(1024)S(1)}, f32[2048]{0:T(1024)}, u32[]{:S(2)}) copy-start(f32[2048]{0:T(1024)} %param.22) | copy-start | bytes 24580
  93.3 1.4 %copy-start.1 = (bf16[768,1024]{1,0:T(8,128)(2,1)S(1)}, bf16[768,1024]{1,0:T(8,128)(2,1)}, u32[]{:S(2)}) copy-start(bf16[768,1024]{1,0:T(8,128)(2,1)} %get-tuple-element.8) | copy-start | bytes 4718596

commit v4 on v2

--- a/solution.py
+++ b/solution.py
@@ -263,7 +263,7 @@
 def history_layer(n, spans, tails, gain, projected, history_in, out_proj):
     rows, width = history_in.shape
     size = width // HEADS
-    row_tile = next(t for t in (256, 128, 64, 32, 16, rows) if rows % t == 0)
+    row_tile = next(t for t in (384, 256, 128, 64, 32, 16, rows) if rows % t == 0)
     smem = pl.BlockSpec(memory_space=pltpu.SMEM)
     anywhere = pl.BlockSpec(memory_space=pl.ANY)
     vmem = pl.BlockSpec(memory_space=pltpu.VMEM)

time: 97.1 us -> 97 us (level)
  no operation moved by 1% of the time
where the time goes in v4:
time: 97 us; the launch traced here: 95.4 us
  Pallas kernels  90.7 us (94%)
  matrix products  1.47 us (2%)
  local copies, waits for them, and re-layouts  1.37 us (1%)
  other arithmetic  1.09 us (1%)
    pallas_call x1, Pallas kernels, history_layer(): pl.pallas_call(functools.partial(history_kernel, n, row_tile), out_shape=...  90.7 us

profile of v4, /device:TPU:3, one launch (start us, length us, event | category | flops | bytes accessed | tf_op | source)
XLA Modules:
  0.0 95.4 jit_solution(1076013658839860968)
XLA Ops:
  0.6 0.0 copy-start
  0.6 0.0 copy-start.2
  0.7 0.0 copy-start.7
  0.7 0.0 copy-start.3
  0.7 0.0 copy-start.4
  0.7 0.0 copy-start.5
  0.7 0.0 copy-start.6
  0.7 90.7 %history_layer.1 = (bf16[768,1024]{1,0:T(8,128)(2,1)}, f32[16,1,1024]{2,1,0:T(1,128)}) custom-call(s32[8]{0:T(128)} %spans_ref.1, s32[8]{0:T(128)} %tails_ref.1, f32[1,1024]{1,0:T(1,128)} %bitcast.6, bf16[768,4096]{1,0:T(8,128)(2,1)} %proj_ref.1, bf16[768,1024]{1,0:T(8,128)(2,1)} %hist_ref.1, bf16[1024,1024]{1,0:T(8,128)(2,1)} %weight_ref.1), custom_call_target="tpu_custom_call" | custom-call | tf_op jit(solution)/shard_map/history_layer/pallas_call | solution.py:270
  91.4 0.9 convert_element_type.16
  92.3 0.0 copy-done.2
  92.3 0.1 select_reduce_fusion.1
  92.4 0.0 copy-done.7
  92.4 0.1 select_reduce_fusion
  92.5 0.3 convolution_convert_fusion
  92.8 0.0 copy-done
  92.8 0.0 copy-done.3
  92.8 0.0 copy-done.4
  92.8 0.0 copy-done.5
  92.8 0.0 copy-done.6
  92.8 0.0 copy-start.1
  92.8 1.2 %fusion.3 = f32[128]{0:T(128)} fusion(bf16[128,2048]{1,0:T(8,128)(2,1)S(1)} %copy-done, bf16[2048,128]{1,0:T(8,128)(2,1)S(1)} %copy-done.3, bf16[128,1024]{1,0:T(8,128)(2,1)S(1)} %copy-done.4, bf16[128,1024]{1,0:T(8,128)(2,1)S(1)} %convolution_convert_fusion, f32[2048]{0:T(1024)S(1)} %copy-done.5, f32[2048]{0:T(1024)S(1)} %copy-done.6), kind=kOutput, calls=%fused_computation.4 | convolution fusion | flops 137641856 | bytes 1589760 | tf_op jit(solution)/shard_map/dot_general | solution.py:334
  94.0 0.2 copy-done.1
  94.2 1.1 %copy.20 = bf16[768,1024]{1,0:T(8,128)(2,1)} copy(bf16[768,1024]{1,0:T(8,128)(2,1)S(1)} %copy-done.1) | data formatting | bytes 3145728
  (1 shorter events, 0.0 us)
Async XLA Ops:
  0.6 92.1 %copy-start = (bf16[128,2048]{1,0:T(8,128)(2,1)S(1)}, bf16[128,2048]{1,0:T(8,128)(2,1)}, u32[]{:S(2)}) copy-start(bf16[128,2048]{1,0:T(8,128)(2,1)} %param.21) | copy-start | bytes 1572868
  0.6 91.6 %copy-start.2 = (s32[8]{0:T(128)S(1)}, s32[8]{0:T(128)}, u32[]{:S(2)}) copy-start(s32[8]{0:T(128)} %spans_ref.1) | copy-start | bytes 100
  0.7 91.7 %copy-start.7 = (s32[128]{0:T(128)S(1)}, s32[128]{0:T(128)}, u32[]{:S(2)}) copy-start(s32[128]{0:T(128)} %param.19) | copy-start | bytes 1540
  0.7 92.1 %copy-start.3 = (bf16[2048,128]{1,0:T(8,128)(2,1)S(1)}, bf16[2048,128]{1,0:T(8,128)(2,1)}, u32[]{:S(2)}) copy-start(bf16[2048,128]{1,0:T(8,128)(2,1)} %param.20) | copy-start | bytes 1572868
  0.7 92.1 %copy-start.4 = (bf16[128,1024]{1,0:T(8,128)(2,1)S(1)}, bf16[128,1024]{1,0:T(8,128)(2,1)}, u32[]{:S(2)}) copy-start(bf16[128,1024]{1,0:T(8,128)(2,1)} %param.18) | copy-start | bytes 786436
  0.7 92.1 %copy-start.5 = (f32[2048]{0:T(1024)S(1)}, f32[2048]{0:T(1024)}, u32[]{:S(2)}) copy-start(f32[2048]{0:T(1024)} %param.23) | copy-start | bytes 24580
  0.7 92.1 %copy-start.6 = (f32[2048]{0:T(1024)S(1)}, f32[2048]{0:T(1024)}, u32[]{:S(2)}) copy-start(f32[2048]{0:T(1024)} %param.22) | copy-start | bytes 24580
  92.8 1.4 %copy-start.1 = (bf16[768,1024]{1,0:T(8,128)(2,1)S(1)}, bf16[768,1024]{1,0:T(8,128)(2,1)}, u32[]{:S(2)}) copy-start(bf16[768,1024]{1,0:T(8,128)(2,1)} %get-tuple-element.8) | copy-start | bytes 4718596
